TPU v7x, 256 devices: a whole 4x4x8 slice. The times are simulated.
256 devices in a mesh: rows: 32 (over z, y), blk: 8 (over x, core).
Axes of the slice: x: 4, y: 4, z: 8, core: 2. Of those that a mesh axis runs over, the one named last changes fastest.
Arguments:
- acol: int32 [512, 32], P('rows', 'blk'), may hold values from -1 to 511, as said below
- aval: bfloat16 [512, 32, 128, 128], P('rows', 'blk'), may hold values from -0.109375 to 0.109375
- mcol: int32 [2, 512, 4], P(None, 'rows'), may hold values from 0 to 255, as said below
- mval: bfloat16 [2, 512, 4, 128, 128], P(None, 'rows'), may hold values from -12 to 12
- rpat: int32 [2, 512, 2], P(None, 'rows'), may hold values from 0 to 255, as said below
- scol: int32 [2, 256], replicated, may hold values from 0 to 511, as said below
- cand: int32 [2, 512, 2], P(None, 'rows'), may hold values from 0 to 255, as said below
Outputs:
- resid: bfloat16 [2, 512, 2, 128, 128], P(None, 'rows', None, None, 'blk')
- scores: float32 [2, 512, 2, 128], P(None, 'rows', None, 'blk')
Inputs may be any that keep to these rules, and one draw needn't show every extreme that they name: `acol`: each block row lists 27 different block columns, each at most 16 block rows from the row itself, counted cyclically modulo 512; its other 5 entries are -1. `mcol`: the entries of one block row in one slab differ. `rpat`: the entries of one block row in one slab differ. `scol`: the entries of one slab differ. `cand`: the entries of one block row in one slab differ.
All inputs are finite; a program needn't handle non-finite values.
Results may differ from a plain program's by a relative error of at most 0.0025.
Values may be sent and summed in bfloat16 or wider, within the bound.
A program may use at most 128 MiB of HBM per device.

v0:
```python
import functools

import jax
import jax.numpy as jnp
from jax import lax
from jax.experimental import pallas as pl
from jax.experimental.pallas import tpu as pltpu
from jax.sharding import PartitionSpec as P

MESH = pl.DeviceIdType.MESH
CORES = 2


def kernel(
    dims,
    scol_s, cand_s, rpat_s, acol_h, mcol_h, rpat_h, aval_h, mval_h,
    o_res, o_sc,
    a_win, m_win, r_win, r_turn, sc_own, ac_v, mc_v, rp_v,
    ac_s, mc_s, rp_s, idx_m, idx_r, diag,
    a_send, a_recv, m_send, m_recv, r_send, r_recv,
    ac_send, ac_recv, mc_send, mc_recv, rp_send, rp_recv,
    o_send, o_recv, s_send, s_recv, loc,
):
    rings, blks, rows, own, per, qm, q2, n = dims
    chips = blks // CORES
    reach = rows
    total = rings * rows
    r, b = lax.axis_index("rows"), lax.axis_index("blk")
    x, t = b // CORES, b % CORES
    up, down = lax.rem(r + 1, rings), lax.rem(r + rings - 1, rings)
    mate = (r, CORES * x + (1 - t))
    mq, rq = own * qm, own * q2
    zero_m, zero_r = m_win.shape[0] - 1, r_win.shape[0] - 1

    def remote(src, dst, send, recv, where):
        return pltpu.make_async_remote_copy(
            src_ref=src, dst_ref=dst, send_sem=send, recv_sem=recv,
            device_id=where, device_id_type=MESH,
        )

    def across(d):
        return lax.rem(x + d, chips)

    def chip(d):
        return CORES * across(d) + t

    home_a = pltpu.make_async_copy(aval_h.at[pl.ds(own * x, own)], a_win.at[b], loc.at[0])
    home_a.start()
    home_m = pltpu.make_async_copy(
        mval_h.at[t], m_win.at[pl.ds(mq * (chips - x), mq * chips)], loc.at[1]
    )
    home_m.start()
    home_ac = pltpu.make_async_copy(acol_h, ac_v.at[b], loc.at[2])
    home_mc = pltpu.make_async_copy(mcol_h.at[t], mc_v.at[1], loc.at[3])
    home_rp = pltpu.make_async_copy(rpat_h.at[t], rp_v.at[1], loc.at[4])
    for copy in (home_ac, home_mc, home_rp):
        copy.start()

    barrier = pltpu.get_barrier_semaphore()
    for d in range(1, blks):
        pl.semaphore_signal(
            barrier, inc=1, device_id=(r, lax.rem(b + d, blks)), device_id_type=MESH
        )
    for ring in (up, down):
        for d in range(chips):
            pl.semaphore_signal(barrier, inc=1, device_id=(ring, chip(d)), device_id_type=MESH)
    m_win[zero_m] = jnp.zeros((n, n), m_win.dtype)
    r_win[zero_r] = jnp.zeros((n, n), r_win.dtype)
    pl.semaphore_wait(barrier, blks - 1 + 2 * chips)

    ints = []
    for d in range(1, blks):
        to = lax.rem(b + d, blks)
        ints.append(remote(acol_h, ac_v.at[b], ac_send.at[d], ac_recv.at[b], (r, to)))
    for k, ring in ((0, up), (2, down)):
        ints.append(remote(mcol_h.at[t], mc_v.at[k], mc_send.at[k], mc_recv.at[k], (ring, b)))
        ints.append(remote(rpat_h.at[t], rp_v.at[k], rp_send.at[k], rp_recv.at[k], (ring, b)))
    for copy in ints:
        copy.start()

    m_out = []
    for j in range(chips):
        src = mval_h.at[t, pl.ds(mq * j, mq)]
        for cond, slot, ring, k in (
            (x <= j, j - x, up, 0),
            (x >= j, 2 * chips + j - x, down, 1),
        ):
            safe = jnp.clip(slot, 0, 2 * chips)
            m_out.append((cond, remote(
                src, m_win.at[pl.ds(mq * safe, mq)], m_send.at[chips * k + j], m_recv.at[safe],
                (ring, b),
            )))
    a_out = {}
    for d in (1, chips - 1) + tuple(range(2, chips - 1)):
        a_out[d] = remote(
            aval_h.at[pl.ds(own * across(d), own)], a_win.at[b],
            a_send.at[d], a_recv.at[b], (r, chip(d)),
        )
        a_out[d].start()
    for cond, copy in m_out:
        pl.when(cond)(copy.start)
    home_a.wait()
    swaps = [remote(a_win.at[b], a_win.at[b], a_send.at[chips], a_recv.at[b], mate)]
    swaps[0].start()

    for copy in (home_ac, home_mc, home_rp):
        copy.wait()
    for d in range(1, blks):
        src = lax.rem(b + d, blks)
        remote(acol_h, ac_v.at[src], ac_send.at[d], ac_recv.at[src], (r, b)).wait_recv()
    for k in (0, 2):
        remote(mcol_h.at[t], mc_v.at[k], mc_send.at[k], mc_recv.at[k], (r, b)).wait_recv()
        remote(rpat_h.at[t], rp_v.at[k], rp_send.at[k], rp_recv.at[k], (r, b)).wait_recv()
    moves = [
        pltpu.make_async_copy(ac_v, ac_s, loc.at[2]),
        pltpu.make_async_copy(mc_v, mc_s, loc.at[3]),
        pltpu.make_async_copy(rp_v, rp_s, loc.at[4]),
    ]
    for copy in moves:
        copy.start()
    for copy in moves:
        copy.wait()

    row0 = own * x
    slots = blks * per

    def table_row(i, carry):
        pats = [rpat_s[t, row0 + i, p] for p in range(q2)]
        cands = [cand_s[t, row0 + i, c] for c in range(q2)]
        for p in range(q2):
            owner = scol_s[t, pats[p]]
            diag[q2 * i + p] = jnp.where(owner == rows * r + row0 + i, 1, 0)

        def table_slot(s, inner):
            col = ac_s[s // per, row0 + i, s % per]
            present = col >= 0
            w = lax.rem(col - rows * r + reach + total, total) - row0
            w = jnp.clip(w, 0, 2 * reach + own - 1)
            rel = w + row0
            side, line = lax.shift_right_logical(rel, rows.bit_length() - 1), rel & (rows - 1)
            mc = [mc_s[side, line, q] for q in range(qm)]
            rp = [rp_s[side, line, q] for q in range(q2)]
            for p in range(q2):
                at_m, at_r = jnp.int32(zero_m), jnp.int32(zero_r)
                for q in range(qm):
                    at_m = jnp.where(present & (mc[q] == pats[p]), w * qm + q, at_m)
                for q in range(q2):
                    at_r = jnp.where(present & (rp[q] == cands[p]), w * q2 + q, at_r)
                idx_m[(i * slots + s) * q2 + p] = at_m
                idx_r[(i * slots + s) * q2 + p] = at_r
            return inner

        return lax.fori_loop(0, slots, table_slot, carry)

    lax.fori_loop(0, own, table_row, 0)

    for k, d in enumerate((1, chips - 1) + tuple(range(2, chips - 1))):
        src = chip(d)
        remote(a_win.at[src], a_win.at[src], a_send.at[d], a_recv.at[src], (r, b)).wait_recv()
        swaps.append(remote(
            a_win.at[src], a_win.at[src], a_send.at[chips + 1 + k], a_recv.at[src], mate
        ))
        swaps[-1].start()
    for d in range(chips):
        src = CORES * across(d) + (1 - t)
        remote(a_win.at[src], a_win.at[src], a_send.at[0], a_recv.at[src], (r, b)).wait_recv()
    home_m.wait()
    for slot in range(2 * chips + 1):
        here = (slot >= chips - x) & (slot < 2 * chips - x)
        got = remote(
            mval_h.at[t, pl.ds(0, mq)], m_win.at[pl.ds(mq * slot, mq)],
            m_send.at[0], m_recv.at[slot], (r, b),
        )
        pl.when(jnp.logical_not(here))(got.wait_recv)

    def product(i, win, table):
        def step(k, acc):
            lhs = jnp.concatenate([a_win[k, i, s] for s in range(per)], axis=1)
            picks = []
            for s in range(per):
                at = (i * slots + k * per + s) * q2
                picks.append(jnp.concatenate([win[table[at + p]] for p in range(q2)], axis=1))
            rhs = jnp.concatenate(picks, axis=0)
            return acc + jnp.dot(lhs, rhs, preferred_element_type=jnp.float32)

        return lax.fori_loop(0, blks, step, jnp.zeros((n, q2 * n), jnp.float32))

    eye = (
        lax.broadcasted_iota(jnp.int32, (n, n), 0) == lax.broadcasted_iota(jnp.int32, (n, n), 1)
    ).astype(jnp.float32)

    def resid_row(i, carry):
        summed = product(i, m_win, idx_m)
        for p in range(q2):
            block = summed[:, n * p:n * (p + 1)] - diag[q2 * i + p].astype(jnp.float32) * eye
            r_win[rq * chips + q2 * i + p] = block.astype(r_win.dtype)
            r_turn[q2 * i + p] = block.T.astype(r_turn.dtype)
        return carry

    lax.fori_loop(0, own, resid_row, 0)

    mine = r_win.at[pl.ds(rq * chips, rq)]
    r_out = []
    for d in (1, chips - 1) + tuple(range(2, chips - 1)):
        slot = chips + x - across(d)
        r_out.append((None, remote(
            mine, r_win.at[pl.ds(rq * slot, rq)], r_send.at[d], r_recv.at[slot], (r, chip(d))
        )))
    for j in range(chips):
        for cond, slot, ring, k in (
            (j <= x, x - j, up, 1),
            (j >= x, 2 * chips + x - j, down, 2),
        ):
            safe = jnp.clip(slot, 0, 2 * chips)
            r_out.append((cond, remote(
                mine, r_win.at[pl.ds(rq * safe, rq)], r_send.at[chips * k + j], r_recv.at[safe],
                (ring, CORES * j + t),
            )))
    for cond, copy in r_out:
        if cond is None:
            copy.start()
        else:
            pl.when(cond)(copy.start)

    width = n // blks
    home_o = pltpu.make_async_copy(
        r_turn.at[:, pl.ds(width * b, width), :], o_res.at[t, pl.ds(rq * x, rq)], loc.at[0]
    )
    home_o.start()
    o_out = []
    for d in range(1, blks):
        to = lax.rem(b + d, blks)
        o_out.append(remote(
            r_turn.at[:, pl.ds(width * to, width), :], o_res.at[t, pl.ds(rq * x, rq)],
            o_send.at[d], o_recv.at[b], (r, to),
        ))
        o_out[-1].start()

    for slot in range(2 * chips + 1):
        if slot != chips:
            remote(
                mine, r_win.at[pl.ds(rq * slot, rq)], r_send.at[0], r_recv.at[slot], (r, b)
            ).wait_recv()

    def score_row(i, carry):
        proj = product(i, r_win, idx_r)
        means = jnp.sum(proj * proj, axis=0, keepdims=True) * (1.0 / n)
        for c in range(q2):
            sc_own[pl.ds(q2 * i + c, 1), :] = means[:, n * c:n * (c + 1)]
        return carry

    lax.fori_loop(0, own, score_row, 0)

    home_s = pltpu.make_async_copy(sc_own, o_sc.at[t, x], loc.at[1])
    home_s.start()
    s_out = []
    for d in range(1, blks):
        to = lax.rem(b + d, blks)
        s_out.append(remote(
            sc_own, o_sc.at[t, x], s_send.at[d], s_recv.at[b], (r, to)
        ))
        s_out[-1].start()

    for d in range(1, blks):
        src = lax.rem(b + d, blks)
        sx, st = src // CORES, src % CORES
        remote(
            r_turn.at[:, pl.ds(0, width), :], o_res.at[st, pl.ds(rq * sx, rq)],
            o_send.at[d], o_recv.at[src], (r, b),
        ).wait_recv()
        remote(sc_own, o_sc.at[st, sx], s_send.at[d], s_recv.at[src], (r, b)).wait_recv()
    home_o.wait()
    home_s.wait()
    for copy in ints + list(a_out.values()) + swaps + o_out + s_out:
        copy.wait_send()
    for cond, copy in m_out + r_out:
        if cond is None:
            copy.wait_send()
        else:
            pl.when(cond)(copy.wait_send)


def on_device(rings, blks, acol, aval, mcol, mval, rpat, scol, cand):
    rows, per, n, _ = aval.shape
    slabs, _, qm = mcol.shape
    q2 = rpat.shape[2]
    chips = blks // CORES
    own = rows // chips
    window = 2 * rows + own
    dims = (rings, blks, rows, own, per, qm, q2, n)
    width = n // blks
    smem = pl.BlockSpec(memory_space=pltpu.SMEM)
    anywhere = pl.BlockSpec(memory_space=pl.ANY)
    dma = pltpu.SemaphoreType.DMA
    slots = blks * per
    res, sc = pl.pallas_call(
        functools.partial(kernel, dims),
        out_shape=(
            jax.ShapeDtypeStruct((slabs, rows * q2, width, n), jnp.bfloat16),
            jax.ShapeDtypeStruct((slabs, chips, own * q2, n), jnp.float32),
        ),
        in_specs=[smem] * 3 + [anywhere] * 5,
        out_specs=(anywhere, anywhere),
        scratch_shapes=[
            pltpu.VMEM((blks, own, per, n, n), jnp.bfloat16),
            pltpu.VMEM((window * qm + 1, n, n), jnp.bfloat16),
            pltpu.VMEM((window * q2 + 1, n, n), jnp.bfloat16),
            pltpu.VMEM((own * q2, n, n), jnp.bfloat16),
            pltpu.VMEM((own * q2, n), jnp.float32),
            pltpu.VMEM((blks, rows, per), jnp.int32),
            pltpu.VMEM((3, rows, qm), jnp.int32),
            pltpu.VMEM((3, rows, q2), jnp.int32),
            pltpu.SMEM((blks, rows, per), jnp.int32),
            pltpu.SMEM((3, rows, qm), jnp.int32),
            pltpu.SMEM((3, rows, q2), jnp.int32),
            pltpu.SMEM((own * slots * q2,), jnp.int32),
            pltpu.SMEM((own * slots * q2,), jnp.int32),
            pltpu.SMEM((own * q2,), jnp.int32),
            dma((2 * chips,)), dma((blks,)),
            dma((2 * chips,)), dma((2 * chips + 1,)),
            dma((3 * chips,)), dma((2 * chips + 1,)),
            dma((blks,)), dma((blks,)), dma((3,)), dma((3,)), dma((3,)), dma((3,)),
            dma((blks,)), dma((blks,)), dma((blks,)), dma((blks,)), dma((5,)),
        ],
        compiler_params=pltpu.CompilerParams(
            collective_id=0, has_side_effects=True, vmem_limit_bytes=40 * 2**20
        ),
    )(
        scol, cand, rpat, acol, mcol, rpat, aval,
        mval.reshape(slabs, rows * qm, n, n),
    )
    start = lax.axis_index("blk") * width
    resid = res.reshape(slabs, rows, q2, width, n).swapaxes(3, 4)
    scores = lax.dynamic_slice_in_dim(sc, start, width, 3).reshape(slabs, rows, q2, width)
    return resid, scores


def solution(mesh):
    placed = (
        P("rows", "blk"),
        P("rows", "blk", None, None),
        P(None, "rows", None),
        P(None, "rows", None, None, None),
        P(None, "rows", None),
        P(),
        P(None, "rows", None),
    )
    return jax.shard_map(
        functools.partial(on_device, mesh.shape["rows"], mesh.shape["blk"]),
        mesh=mesh,
        in_specs=placed,
        out_specs=(P(None, "rows", None, None, "blk"), P(None, "rows", None, "blk")),
        check_vma=False,
    )
```

profile of v0, /device:TPU:1, one launch (start us, length us, event | category | flops | bytes accessed | tf_op | source)
XLA Modules:
  0.0 116.4 jit_solution(1141839533091186852)
XLA Ops:
  0.6 0.8 copy.10.rpat_s.rpat_h
  1.4 0.8 copy.12.mcol_h
  2.2 0.8 copy.9.cand_s
  2.9 0.8 copy.11.acol_h
  3.7 0.0 copy-start
  3.7 2.2 %copy-done = bf16[2,16,4,128,128]{4,3,2,1,0:T(8,128)(2,1)S(1)} copy-done((bf16[2,16,4,128,128]{4,3,2,1,0:T(8,128)(2,1)S(1)}, bf16[2,16,4,128,128]{4,3,2,1,0:T(8,128)(2,1)}, u32[]{:S(2)}) %copy-start) | copy-done | bytes 4194328
  5.9 0.0 copy-start.1
  5.9 1.6 %copy-done.1 = bf16[16,4,128,128]{3,2,1,0:T(8,128)(2,1)S(1)} copy-done((bf16[16,4,128,128]{3,2,1,0:T(8,128)(2,1)S(1)}, bf16[16,4,128,128]{3,2,1,0:T(8,128)(2,1)}, u32[]{:S(2)}) %copy-start.1) | copy-done | bytes 2097176
  7.5 0.0 copy-start.2
  7.5 0.7 copy-done.2
  8.2 106.9 %shard_map.86 = (bf16[2,32,16,128]{3,2,1,0:T(8,128)(2,1)S(1)}, f32[2,4,8,128]{3,2,1,0:T(8,128)S(1)}) custom-call(s32[2,256]{1,0:T(2,128)S(1)} %copy-done.2, s32[2,16,2]{2,1,0:T(8,128)S(1)} %copy.9.cand_s, s32[2,16,2]{2,1,0:T(8,128)S(1)} %copy.10.rpat_s.rpat_h, s32[16,4]{1,0:T(8,128)S(1)} %copy.11.acol_h, s32[2,16,4]{2,1,0:T(8,128)S(1)} %copy.12.mcol_h, ...), custom_call_target="tpu_custom_call" | custom-call | tf_op jit(solution)/shard_map/pallas_call | solution.py:296
  115.0 0.7 constant_dynamic-slice_fusion
  115.7 0.7 copy.15
Async XLA Ops:
  3.7 2.2 %copy-start = (bf16[2,16,4,128,128]{4,3,2,1,0:T(8,128)(2,1)S(1)}, bf16[2,16,4,128,128]{4,3,2,1,0:T(8,128)(2,1)}, u32[]{:S(2)}) copy-start(bf16[2,16,4,128,128]{4,3,2,1,0:T(8,128)(2,1)} %param.10) | copy-start | bytes 12582916
  5.9 1.6 %copy-start.1 = (bf16[16,4,128,128]{3,2,1,0:T(8,128)(2,1)S(1)}, bf16[16,4,128,128]{3,2,1,0:T(8,128)(2,1)}, u32[]{:S(2)}) copy-start(bf16[16,4,128,128]{3,2,1,0:T(8,128)(2,1)} %aval_h.1) | copy-start | bytes 6291460
  7.5 0.7 copy-start.2
where the time goes:
time: 117 us; the launch traced here: 116 us
  Pallas kernels  107 us (91%)
  local copies, waits for them, and re-layouts  8.91 us (8%)
    pallas_call x1, Pallas kernels, on_device(): pl.pallas_call(functools.partial(kernel, dims), out_shape=(jax.ShapeDtype...  107 us
    unnamed x11, local copies, waits for them, and re-layouts  8.21 us

commit v1 on v0

--- a/solution.py
+++ b/solution.py
@@ -13,13 +13,13 @@
 
 def kernel(
     dims,
-    scol_s, cand_s, rpat_s, acol_h, mcol_h, rpat_h, aval_h, mval_h,
+    scol_h, cand_h, rpat_h, acol_h, mcol_h, aval_h, mval_h,
     o_res, o_sc,
     a_win, m_win, r_win, r_turn, sc_own, ac_v, mc_v, rp_v,
-    ac_s, mc_s, rp_s, idx_m, idx_r, diag,
+    ac_s, mc_s, rp_s, scol_s, cand_s, idx_m, idx_r, diag,
     a_send, a_recv, m_send, m_recv, r_send, r_recv,
     ac_send, ac_recv, mc_send, mc_recv, rp_send, rp_recv,
-    o_send, o_recv, s_send, s_recv, loc,
+    o_send, o_recv, s_send, s_recv, h_send, h_recv, loc,
 ):
     rings, blks, rows, own, per, qm, q2, n = dims
     chips = blks // CORES
@@ -45,28 +45,27 @@
         return CORES * across(d) + t
 
     home_a = pltpu.make_async_copy(aval_h.at[pl.ds(own * x, own)], a_win.at[b], loc.at[0])
-    home_a.start()
     home_m = pltpu.make_async_copy(
         mval_h.at[t], m_win.at[pl.ds(mq * (chips - x), mq * chips)], loc.at[1]
     )
-    home_m.start()
     home_ac = pltpu.make_async_copy(acol_h, ac_v.at[b], loc.at[2])
     home_mc = pltpu.make_async_copy(mcol_h.at[t], mc_v.at[1], loc.at[3])
     home_rp = pltpu.make_async_copy(rpat_h.at[t], rp_v.at[1], loc.at[4])
-    for copy in (home_ac, home_mc, home_rp):
-        copy.start()
+    home_sc = pltpu.make_async_copy(scol_h, scol_s, loc.at[5])
+    home_ca = pltpu.make_async_copy(cand_h, cand_s, loc.at[6])
 
     barrier = pltpu.get_barrier_semaphore()
+    for ring in (up, down):
+        pl.semaphore_signal(barrier, inc=1, device_id=(ring, b), device_id_type=MESH)
     for d in range(1, blks):
         pl.semaphore_signal(
             barrier, inc=1, device_id=(r, lax.rem(b + d, blks)), device_id_type=MESH
         )
-    for ring in (up, down):
-        for d in range(chips):
-            pl.semaphore_signal(barrier, inc=1, device_id=(ring, chip(d)), device_id_type=MESH)
+    for copy in (home_ac, home_mc, home_rp, home_sc, home_ca, home_a, home_m):
+        copy.start()
     m_win[zero_m] = jnp.zeros((n, n), m_win.dtype)
     r_win[zero_r] = jnp.zeros((n, n), r_win.dtype)
-    pl.semaphore_wait(barrier, blks - 1 + 2 * chips)
+    pl.semaphore_wait(barrier, blks - 1 + 2)
 
     ints = []
     for d in range(1, blks):
@@ -78,18 +77,20 @@
     for copy in ints:
         copy.start()
 
+    last = chips - 1
     m_out = []
-    for j in range(chips):
-        src = mval_h.at[t, pl.ds(mq * j, mq)]
-        for cond, slot, ring, k in (
-            (x <= j, j - x, up, 0),
-            (x >= j, 2 * chips + j - x, down, 1),
+    for k in range(chips):
+        for cond, j, slot, ring, side in (
+            ((x <= last - k) & ((x > 0) | (k > 0)), last - k, last - k - x, up, 0),
+            ((x >= k) & ((x < last) | (k > 0)), k, 2 * chips + k - x, down, 1),
         ):
             safe = jnp.clip(slot, 0, 2 * chips)
             m_out.append((cond, remote(
-                src, m_win.at[pl.ds(mq * safe, mq)], m_send.at[chips * k + j], m_recv.at[safe],
-                (ring, b),
+                mval_h.at[t, pl.ds(mq * j, mq)], m_win.at[pl.ds(mq * safe, mq)],
+                m_send.at[chips * side + k], m_recv.at[safe], (ring, b),
             )))
+    for cond, copy in m_out:
+        pl.when(cond)(copy.start)
     a_out = {}
     for d in (1, chips - 1) + tuple(range(2, chips - 1)):
         a_out[d] = remote(
@@ -97,13 +98,11 @@
             a_send.at[d], a_recv.at[b], (r, chip(d)),
         )
         a_out[d].start()
-    for cond, copy in m_out:
-        pl.when(cond)(copy.start)
     home_a.wait()
     swaps = [remote(a_win.at[b], a_win.at[b], a_send.at[chips], a_recv.at[b], mate)]
     swaps[0].start()
 
-    for copy in (home_ac, home_mc, home_rp):
+    for copy in (home_ac, home_mc, home_rp, home_sc, home_ca):
         copy.wait()
     for d in range(1, blks):
         src = lax.rem(b + d, blks)
@@ -125,21 +124,21 @@
     slots = blks * per
 
     def table_row(i, carry):
-        pats = [rpat_s[t, row0 + i, p] for p in range(q2)]
-        cands = [cand_s[t, row0 + i, c] for c in range(q2)]
+        pats = [rp_s[1, p, row0 + i] for p in range(q2)]
+        cands = [cand_s[t, c, row0 + i] for c in range(q2)]
         for p in range(q2):
             owner = scol_s[t, pats[p]]
             diag[q2 * i + p] = jnp.where(owner == rows * r + row0 + i, 1, 0)
 
         def table_slot(s, inner):
-            col = ac_s[s // per, row0 + i, s % per]
+            col = ac_s[s // per, s % per, row0 + i]
             present = col >= 0
             w = lax.rem(col - rows * r + reach + total, total) - row0
             w = jnp.clip(w, 0, 2 * reach + own - 1)
             rel = w + row0
             side, line = lax.shift_right_logical(rel, rows.bit_length() - 1), rel & (rows - 1)
-            mc = [mc_s[side, line, q] for q in range(qm)]
-            rp = [rp_s[side, line, q] for q in range(q2)]
+            mc = [mc_s[side, q, line] for q in range(qm)]
+            rp = [rp_s[side, q, line] for q in range(q2)]
             for p in range(q2):
                 at_m, at_r = jnp.int32(zero_m), jnp.int32(zero_r)
                 for q in range(qm):
@@ -153,6 +152,26 @@
         return lax.fori_loop(0, slots, table_slot, carry)
 
     lax.fori_loop(0, own, table_row, 0)
+
+    odd = lax.rem(x, 2) == 1
+    half, hb = x // 2, mq // 2
+    src_slot = jnp.where(odd, last - x, 2 * chips - x)
+    dst_slot = jnp.where(odd, last, chips + 1)
+    dst_chip = jnp.where(odd, 0, last)
+
+    def m_wait(slot):
+        remote(
+            mval_h.at[t, pl.ds(0, mq)], m_win.at[pl.ds(mq * slot, mq)],
+            m_send.at[0], m_recv.at[slot], (r, b),
+        ).wait_recv()
+
+    m_wait(src_slot)
+    relay = remote(
+        m_win.at[pl.ds(mq * src_slot + hb * half, hb)],
+        m_win.at[pl.ds(mq * dst_slot + hb * half, hb)],
+        h_send.at[0], h_recv.at[half], (r, CORES * dst_chip + t),
+    )
+    relay.start()
 
     for k, d in enumerate((1, chips - 1) + tuple(range(2, chips - 1))):
         src = chip(d)
@@ -165,25 +184,31 @@
         src = CORES * across(d) + (1 - t)
         remote(a_win.at[src], a_win.at[src], a_send.at[0], a_recv.at[src], (r, b)).wait_recv()
     home_m.wait()
+    edge = (x == 0) | (x == last)
+    far = jnp.where(x == 0, last, chips + 1)
     for slot in range(2 * chips + 1):
         here = (slot >= chips - x) & (slot < 2 * chips - x)
-        got = remote(
-            mval_h.at[t, pl.ds(0, mq)], m_win.at[pl.ds(mq * slot, mq)],
-            m_send.at[0], m_recv.at[slot], (r, b),
-        )
-        pl.when(jnp.logical_not(here))(got.wait_recv)
+        skip = here | (slot == src_slot) | (edge & (slot == far))
+        pl.when(jnp.logical_not(skip))(functools.partial(m_wait, slot))
+
+    @pl.when(edge)
+    def _():
+        for h in range(2):
+            part = m_win.at[pl.ds(mq * far + hb * h, hb)]
+            remote(part, part, h_send.at[0], h_recv.at[h], (r, b)).wait_recv()
 
     def product(i, win, table):
-        def step(k, acc):
+        acc = None
+        for k in range(blks):
             lhs = jnp.concatenate([a_win[k, i, s] for s in range(per)], axis=1)
             picks = []
             for s in range(per):
                 at = (i * slots + k * per + s) * q2
                 picks.append(jnp.concatenate([win[table[at + p]] for p in range(q2)], axis=1))
             rhs = jnp.concatenate(picks, axis=0)
-            return acc + jnp.dot(lhs, rhs, preferred_element_type=jnp.float32)
-
-        return lax.fori_loop(0, blks, step, jnp.zeros((n, q2 * n), jnp.float32))
+            part = jnp.dot(lhs, rhs, preferred_element_type=jnp.float32)
+            acc = part if acc is None else acc + part
+        return acc
 
     eye = (
         lax.broadcasted_iota(jnp.int32, (n, n), 0) == lax.broadcasted_iota(jnp.int32, (n, n), 1)
@@ -197,30 +222,45 @@
             r_turn[q2 * i + p] = block.T.astype(r_turn.dtype)
         return carry
 
-    lax.fori_loop(0, own, resid_row, 0)
-
-    mine = r_win.at[pl.ds(rq * chips, rq)]
-    r_out = []
-    for d in (1, chips - 1) + tuple(range(2, chips - 1)):
-        slot = chips + x - across(d)
-        r_out.append((None, remote(
-            mine, r_win.at[pl.ds(rq * slot, rq)], r_send.at[d], r_recv.at[slot], (r, chip(d))
-        )))
-    for j in range(chips):
-        for cond, slot, ring, k in (
-            (j <= x, x - j, up, 1),
-            (j >= x, 2 * chips + x - j, down, 2),
-        ):
-            safe = jnp.clip(slot, 0, 2 * chips)
-            r_out.append((cond, remote(
-                mine, r_win.at[pl.ds(rq * safe, rq)], r_send.at[chips * k + j], r_recv.at[safe],
-                (ring, CORES * j + t),
-            )))
-    for cond, copy in r_out:
+    left, right = lax.rem(x + last, chips), lax.rem(x + 1, chips)
+    by_left, by_right = (r, CORES * left + t), (r, CORES * right + t)
+    above, below = (up, b), (down, b)
+    rh = rq // 2
+    r_all = []
+
+    def piece(slot, h):
+        return r_win.at[pl.ds(rq * slot + rh * h, rh)]
+
+    def give(slot, h, to_slot, where, cond=None):
+        if cond is not None:
+            to_slot = jnp.clip(to_slot, 0, 2 * chips)
+        copy = remote(
+            piece(slot, h), piece(to_slot, h), r_send.at[len(r_all)],
+            r_recv.at[2 * to_slot + h], where,
+        )
+        r_all.append((cond, copy))
         if cond is None:
             copy.start()
         else:
             pl.when(cond)(copy.start)
+
+    def take(slot, h, cond=None):
+        def wait():
+            remote(
+                piece(slot, h), piece(slot, h), r_send.at[0], r_recv.at[2 * slot + h], (r, b)
+            ).wait_recv()
+
+        if cond is None:
+            wait()
+        else:
+            pl.when(cond)(wait)
+
+    for h in range(2):
+        lax.fori_loop(own // 2 * h, own // 2 * (h + 1), resid_row, 0)
+        give(chips, h, chips + x - right, by_right)
+        give(chips, h, chips + x - left, by_left)
+        give(chips, h, 0, above)
+        give(chips, h, 2 * chips, below)
 
     width = n // blks
     home_o = pltpu.make_async_copy(
@@ -236,11 +276,32 @@
         ))
         o_out[-1].start()
 
-    for slot in range(2 * chips + 1):
-        if slot != chips:
-            remote(
-                mine, r_win.at[pl.ds(rq * slot, rq)], r_send.at[0], r_recv.at[slot], (r, b)
-            ).wait_recv()
+    at_left, at_right = chips + left - x, chips + right - x
+    for h in range(2):
+        take(at_left, h)
+        if h == 0:
+            give(at_left, h, chips + left - right, by_right)
+        give(at_left, h, 2 * chips - 1, below, x >= 1)
+        take(at_right, h)
+        if h == 1:
+            give(at_right, h, chips + right - left, by_left)
+        give(at_right, h, 1, above, x <= last - 1)
+        take(0, h)
+        give(0, h, last, by_right, x == last)
+        take(2 * chips, h)
+        give(2 * chips, h, chips + 1, by_left, x == 0)
+    inner = (x >= 1) & (x <= last - 1)
+    for h in range(2):
+        take(1, h, x <= last - 1)
+        give(1, h, 2, by_left, inner)
+        take(2 * chips - 1, h, x >= 1)
+        give(2 * chips - 1, h, 2 * chips - 2, by_right, inner)
+    for h in range(2):
+        take(jnp.where(x < 2, chips + 2, chips - 2), h)
+        take(2, h, x < 2)
+        take(3, h, x == 0)
+        take(2 * chips - 2, h, x >= 2)
+        take(chips + 1, h, x == last)
 
     def score_row(i, carry):
         proj = product(i, r_win, idx_r)
@@ -271,9 +332,9 @@
         remote(sc_own, o_sc.at[st, sx], s_send.at[d], s_recv.at[src], (r, b)).wait_recv()
     home_o.wait()
     home_s.wait()
-    for copy in ints + list(a_out.values()) + swaps + o_out + s_out:
+    for copy in ints + list(a_out.values()) + swaps + [relay] + o_out + s_out:
         copy.wait_send()
-    for cond, copy in m_out + r_out:
+    for cond, copy in m_out + r_all:
         if cond is None:
             copy.wait_send()
         else:
@@ -289,7 +350,6 @@
     window = 2 * rows + own
     dims = (rings, blks, rows, own, per, qm, q2, n)
     width = n // blks
-    smem = pl.BlockSpec(memory_space=pltpu.SMEM)
     anywhere = pl.BlockSpec(memory_space=pl.ANY)
     dma = pltpu.SemaphoreType.DMA
     slots = blks * per
@@ -299,7 +359,7 @@
             jax.ShapeDtypeStruct((slabs, rows * q2, width, n), jnp.bfloat16),
             jax.ShapeDtypeStruct((slabs, chips, own * q2, n), jnp.float32),
         ),
-        in_specs=[smem] * 3 + [anywhere] * 5,
+        in_specs=[anywhere] * 7,
         out_specs=(anywhere, anywhere),
         scratch_shapes=[
             pltpu.VMEM((blks, own, per, n, n), jnp.bfloat16),
@@ -307,26 +367,29 @@
             pltpu.VMEM((window * q2 + 1, n, n), jnp.bfloat16),
             pltpu.VMEM((own * q2, n, n), jnp.bfloat16),
             pltpu.VMEM((own * q2, n), jnp.float32),
-            pltpu.VMEM((blks, rows, per), jnp.int32),
-            pltpu.VMEM((3, rows, qm), jnp.int32),
-            pltpu.VMEM((3, rows, q2), jnp.int32),
-            pltpu.SMEM((blks, rows, per), jnp.int32),
-            pltpu.SMEM((3, rows, qm), jnp.int32),
-            pltpu.SMEM((3, rows, q2), jnp.int32),
+            pltpu.VMEM((blks, per, rows), jnp.int32),
+            pltpu.VMEM((3, qm, rows), jnp.int32),
+            pltpu.VMEM((3, q2, rows), jnp.int32),
+            pltpu.SMEM((blks, per, rows), jnp.int32),
+            pltpu.SMEM((3, qm, rows), jnp.int32),
+            pltpu.SMEM((3, q2, rows), jnp.int32),
+            pltpu.SMEM(scol.shape, jnp.int32),
+            pltpu.SMEM((slabs, q2, rows), jnp.int32),
             pltpu.SMEM((own * slots * q2,), jnp.int32),
             pltpu.SMEM((own * slots * q2,), jnp.int32),
             pltpu.SMEM((own * q2,), jnp.int32),
             dma((2 * chips,)), dma((blks,)),
             dma((2 * chips,)), dma((2 * chips + 1,)),
-            dma((3 * chips,)), dma((2 * chips + 1,)),
+            dma((26,)), dma((4 * chips + 2,)),
             dma((blks,)), dma((blks,)), dma((3,)), dma((3,)), dma((3,)), dma((3,)),
-            dma((blks,)), dma((blks,)), dma((blks,)), dma((blks,)), dma((5,)),
+            dma((blks,)), dma((blks,)), dma((blks,)), dma((blks,)),
+            dma((1,)), dma((2,)), dma((7,)),
         ],
         compiler_params=pltpu.CompilerParams(
-            collective_id=0, has_side_effects=True, vmem_limit_bytes=40 * 2**20
+            collective_id=0, has_side_effects=True, vmem_limit_bytes=67043328
         ),
     )(
-        scol, cand, rpat, acol, mcol, rpat, aval,
+        scol, cand.swapaxes(1, 2), rpat.swapaxes(1, 2), acol.T, mcol.swapaxes(1, 2), aval,
         mval.reshape(slabs, rows * qm, n, n),
     )
     start = lax.axis_index("blk") * width

time: 117 us -> 79.1 us (0.68)
  Pallas kernels: 107 us -> 75.2 us
  local copies, waits for them, and re-layouts: 8.91 us -> 3.13 us
    pallas_call x1, Pallas kernels: 107 us -> 75.2 us  [on_device(): pl.pallas_call(functools.partial(kernel, dims), out_shape=(jax.ShapeDtype...]
    unnamed x11 -> x1, local copies, waits for them, and re-layouts: 8.21 us -> 1.67 us
where the time goes in v1:
time: 79.1 us; the launch traced here: 78.9 us
  Pallas kernels  75.2 us (95%)
  local copies, waits for them, and re-layouts  3.13 us (4%)
    pallas_call x1, Pallas kernels, on_device(): pl.pallas_call(functools.partial(kernel, dims), out_shape=(jax.ShapeDtype...  75.2 us
    unnamed x1, local copies, waits for them, and re-layouts  1.67 us

profile of v1, /device:TPU:1, one launch (start us, length us, event | category | flops | bytes accessed | tf_op | source)
XLA Modules:
  0.0 78.9 jit_solution(12207831818154651532)
XLA Ops:
  0.6 75.2 %shard_map.86 = (bf16[2,32,16,128]{3,2,1,0:T(8,128)(2,1)}, f32[2,4,8,128]{3,2,1,0:T(8,128)}) custom-call(s32[2,256]{1,0:T(2,128)} %scol_h.1, s32[2,2,16]{2,1,0:T(2,128)} %bitcast.13, s32[2,2,16]{2,1,0:T(2,128)} %bitcast.14, s32[4,16]{1,0:T(4,128)} %bitcast.15, s32[2,4,16]{2,1,0:T(4,128)} %bitcast.12, bf16[16,4,128,128]{3,2,1,0:T(8,128)(2,1)} %aval_h.1, ...), custom_call_target="tpu_custom_call" | custom-call | tf_op jit(solution)/shard_map/pallas_call | solution.py:356
  75.8 1.5 %constant_dynamic-slice_fusion = f32[2,4,8,16]{3,2,1,0:T(8,128)} fusion(f32[2,4,8,128]{3,2,1,0:T(8,128)} %get-tuple-element.5, s32[]{:T(128)S(6)} %select_n.3), kind=kLoop, calls=%fused_computation | loop fusion | bytes 8196 | tf_op jit(solution)/shard_map/dynamic_slice | solution.py:397
  77.3 1.7 %copy.10 = bf16[2,16,2,128,16]{3,4,2,1,0:T(8,128)(2,1)} copy(bf16[2,16,2,128,16]{3,4,2,1,0:T(8,128)(2,1)} %bitcast.10) | data formatting | bytes 524288

commit v2 on v1

--- a/solution.py
+++ b/solution.py
@@ -79,28 +79,50 @@
 
     last = chips - 1
     m_out = []
+    mh, hr = mq // 2, own // 2
     for k in range(chips):
-        for cond, j, slot, ring, side in (
-            ((x <= last - k) & ((x > 0) | (k > 0)), last - k, last - k - x, up, 0),
-            ((x >= k) & ((x < last) | (k > 0)), k, 2 * chips + k - x, down, 1),
-        ):
-            safe = jnp.clip(slot, 0, 2 * chips)
-            m_out.append((cond, remote(
-                mval_h.at[t, pl.ds(mq * j, mq)], m_win.at[pl.ds(mq * safe, mq)],
-                m_send.at[chips * side + k], m_recv.at[safe], (ring, b),
-            )))
+        for e in range(2):
+            for cond, skip, j, h, slot, ring in (
+                (x <= last - k, ((1, 0), (0, 0), (0, 1), (0, 2)), last - k, 1 - e, last - k - x, up),
+                (x >= k, ((last - 1, 0), (last, 0), (last, 1), (last, 2)), k, e,
+                 2 * chips + k - x, down),
+            ):
+                if k == 0 and e == 0:
+                    cond &= (x != skip[0][0]) & (x != skip[1][0])
+                elif k == 0 or (k == 1 and e == 0):
+                    cond &= x != skip[1][0]
+                safe = jnp.clip(slot, 0, 2 * chips)
+                m_out.append((cond, remote(
+                    mval_h.at[t, pl.ds(mq * j + mh * h, mh)],
+                    m_win.at[pl.ds(mq * safe + mh * h, mh)],
+                    m_send.at[len(m_out)], m_recv.at[2 * safe + h], (ring, b),
+                )))
     for cond, copy in m_out:
         pl.when(cond)(copy.start)
-    a_out = {}
-    for d in (1, chips - 1) + tuple(range(2, chips - 1)):
-        a_out[d] = remote(
-            aval_h.at[pl.ds(own * across(d), own)], a_win.at[b],
-            a_send.at[d], a_recv.at[b], (r, chip(d)),
+    hops = (1, chips - 1) + tuple(range(2, chips - 1))
+    a_all = []
+
+    def a_part(src, g):
+        return a_win.at[src, pl.ds(hr * g, hr)]
+
+    def a_copy(source, src, g, where):
+        copy = remote(
+            source, a_part(src, g), a_send.at[len(a_all)], a_recv.at[blks * g + src], where
         )
-        a_out[d].start()
+        copy.start()
+        a_all.append(copy)
+
+    def a_wait(src, g):
+        remote(
+            a_part(src, g), a_part(src, g), a_send.at[0], a_recv.at[blks * g + src], (r, b)
+        ).wait_recv()
+
+    for g in range(2):
+        for d in hops:
+            a_copy(aval_h.at[pl.ds(own * across(d) + hr * g, hr)], b, g, (r, chip(d)))
     home_a.wait()
-    swaps = [remote(a_win.at[b], a_win.at[b], a_send.at[chips], a_recv.at[b], mate)]
-    swaps[0].start()
+    for g in range(2):
+        a_copy(a_part(b, g), b, g, mate)
 
     for copy in (home_ac, home_mc, home_rp, home_sc, home_ca):
         copy.wait()
@@ -153,49 +175,78 @@
 
     lax.fori_loop(0, own, table_row, 0)
 
-    odd = lax.rem(x, 2) == 1
-    half, hb = x // 2, mq // 2
-    src_slot = jnp.where(odd, last - x, 2 * chips - x)
-    dst_slot = jnp.where(odd, last, chips + 1)
-    dst_chip = jnp.where(odd, 0, last)
-
-    def m_wait(slot):
-        remote(
-            mval_h.at[t, pl.ds(0, mq)], m_win.at[pl.ds(mq * slot, mq)],
-            m_send.at[0], m_recv.at[slot], (r, b),
-        ).wait_recv()
-
-    m_wait(src_slot)
-    relay = remote(
-        m_win.at[pl.ds(mq * src_slot + hb * half, hb)],
-        m_win.at[pl.ds(mq * dst_slot + hb * half, hb)],
-        h_send.at[0], h_recv.at[half], (r, CORES * dst_chip + t),
-    )
-    relay.start()
-
-    for k, d in enumerate((1, chips - 1) + tuple(range(2, chips - 1))):
-        src = chip(d)
-        remote(a_win.at[src], a_win.at[src], a_send.at[d], a_recv.at[src], (r, b)).wait_recv()
-        swaps.append(remote(
-            a_win.at[src], a_win.at[src], a_send.at[chips + 1 + k], a_recv.at[src], mate
-        ))
-        swaps[-1].start()
-    for d in range(chips):
-        src = CORES * across(d) + (1 - t)
-        remote(a_win.at[src], a_win.at[src], a_send.at[0], a_recv.at[src], (r, b)).wait_recv()
+    left, right = lax.rem(x + last, chips), lax.rem(x + 1, chips)
+    by_left, by_right = (r, CORES * left + t), (r, CORES * right + t)
+    above, below = (up, b), (down, b)
+    inner = (x >= 1) & (x <= last - 1)
+
+    def m_rows(slot, first, count):
+        return m_win.at[pl.ds(mq * slot + qm * first, qm * count)]
+
+    def m_take(slot, h):
+        part = m_rows(slot, hr * h, hr)
+        remote(part, part, m_send.at[0], m_recv.at[2 * slot + h], (r, b)).wait_recv()
+
+    relays = []
+    for cond, needs, slots_of, rows_of, sem, where in (
+        (x == last, ((0, 1), (0, 0)), (0, last), (1, own - 1), h_recv.at[1], by_right),
+        (x == 0, ((2 * chips, 0), (2 * chips, 1)), (2 * chips, chips + 1), (0, own - 1),
+         h_recv.at[1], by_left),
+        (x == 1, ((2, 0),), (2, last), (0, 1), h_recv.at[0], by_left),
+        (x == last - 1, ((2 * chips - 2, 1),), (2 * chips - 2, chips + 1), (own - 1, 1),
+         h_recv.at[0], by_right),
+        (inner, ((1, 1),), (1, 2), (hr, hr), m_recv.at[2 * 2 + 1], by_left),
+        (inner, ((2 * chips - 1, 0),), (2 * chips - 1, 2 * chips - 2), (0, hr),
+         m_recv.at[2 * (2 * chips - 2)], by_right),
+    ):
+        copy = remote(
+            m_rows(slots_of[0], *rows_of), m_rows(slots_of[1], *rows_of),
+            h_send.at[len(relays)], sem, where,
+        )
+        relays.append((cond, copy))
+
+        def pass_on(needs=needs, copy=copy):
+            for slot, h in needs:
+                m_take(slot, h)
+            copy.start()
+
+        pl.when(cond)(pass_on)
+
+    def a_swap(g):
+        for d in hops:
+            a_wait(chip(d), g)
+            a_copy(a_part(chip(d), g), chip(d), g, mate)
+        for d in range(chips):
+            a_wait(CORES * across(d) + (1 - t), g)
+
+    a_swap(0)
     home_m.wait()
     edge = (x == 0) | (x == last)
-    far = jnp.where(x == 0, last, chips + 1)
-    for slot in range(2 * chips + 1):
-        here = (slot >= chips - x) & (slot < 2 * chips - x)
-        skip = here | (slot == src_slot) | (edge & (slot == far))
-        pl.when(jnp.logical_not(skip))(functools.partial(m_wait, slot))
-
-    @pl.when(edge)
-    def _():
-        for h in range(2):
-            part = m_win.at[pl.ds(mq * far + hb * h, hb)]
-            remote(part, part, h_send.at[0], h_recv.at[h], (r, b)).wait_recv()
+    for k in range(chips):
+        for e in range(2):
+            for cond, taken, slot, h in (
+                (
+                    k <= last - x,
+                    ((x == last) & (k == 0)) | ((x == 1) & (k == 2) & (e == 1))
+                    | (inner & (k == 1) & (e == 0)) | ((x == 0) & (k == last)),
+                    k, 1 - e,
+                ),
+                (
+                    k <= x,
+                    ((x == 0) & (k == 0)) | ((x == last - 1) & (k == 2) & (e == 1))
+                    | (inner & (k == 1) & (e == 0)) | ((x == last) & (k == last)),
+                    2 * chips - k, e,
+                ),
+            ):
+                pl.when(cond & jnp.logical_not(taken))(functools.partial(m_take, slot, h))
+
+    def far_take(slot, one, rest):
+        for k, span in ((0, (one, 1)), (1, (rest, own - 1))):
+            part = m_rows(slot, *span)
+            remote(part, part, h_send.at[0], h_recv.at[k], (r, b)).wait_recv()
+
+    pl.when(x == 0)(lambda: far_take(last, 0, 1))
+    pl.when(x == last)(lambda: far_take(chips + 1, own - 1, 0))
 
     def product(i, win, table):
         acc = None
@@ -222,9 +273,6 @@
             r_turn[q2 * i + p] = block.T.astype(r_turn.dtype)
         return carry
 
-    left, right = lax.rem(x + last, chips), lax.rem(x + 1, chips)
-    by_left, by_right = (r, CORES * left + t), (r, CORES * right + t)
-    above, below = (up, b), (down, b)
     rh = rq // 2
     r_all = []
 
@@ -256,25 +304,13 @@
             pl.when(cond)(wait)
 
     for h in range(2):
+        if h == 1:
+            a_swap(1)
         lax.fori_loop(own // 2 * h, own // 2 * (h + 1), resid_row, 0)
         give(chips, h, chips + x - right, by_right)
         give(chips, h, chips + x - left, by_left)
         give(chips, h, 0, above)
         give(chips, h, 2 * chips, below)
-
-    width = n // blks
-    home_o = pltpu.make_async_copy(
-        r_turn.at[:, pl.ds(width * b, width), :], o_res.at[t, pl.ds(rq * x, rq)], loc.at[0]
-    )
-    home_o.start()
-    o_out = []
-    for d in range(1, blks):
-        to = lax.rem(b + d, blks)
-        o_out.append(remote(
-            r_turn.at[:, pl.ds(width * to, width), :], o_res.at[t, pl.ds(rq * x, rq)],
-            o_send.at[d], o_recv.at[b], (r, to),
-        ))
-        o_out[-1].start()
 
     at_left, at_right = chips + left - x, chips + right - x
     for h in range(2):
@@ -290,7 +326,6 @@
         give(0, h, last, by_right, x == last)
         take(2 * chips, h)
         give(2 * chips, h, chips + 1, by_left, x == 0)
-    inner = (x >= 1) & (x <= last - 1)
     for h in range(2):
         take(1, h, x <= last - 1)
         give(1, h, 2, by_left, inner)
@@ -303,6 +338,20 @@
         take(2 * chips - 2, h, x >= 2)
         take(chips + 1, h, x == last)
 
+    width = n // blks
+    home_o = pltpu.make_async_copy(
+        r_turn.at[:, pl.ds(width * b, width), :], o_res.at[t, pl.ds(rq * x, rq)], loc.at[0]
+    )
+    home_o.start()
+    o_out = []
+    for d in range(1, blks):
+        to = lax.rem(b + d, blks)
+        o_out.append(remote(
+            r_turn.at[:, pl.ds(width * to, width), :], o_res.at[t, pl.ds(rq * x, rq)],
+            o_send.at[d], o_recv.at[b], (r, to),
+        ))
+        o_out[-1].start()
+
     def score_row(i, carry):
         proj = product(i, r_win, idx_r)
         means = jnp.sum(proj * proj, axis=0, keepdims=True) * (1.0 / n)
@@ -332,9 +381,9 @@
         remote(sc_own, o_sc.at[st, sx], s_send.at[d], s_recv.at[src], (r, b)).wait_recv()
     home_o.wait()
     home_s.wait()
-    for copy in ints + list(a_out.values()) + swaps + [relay] + o_out + s_out:
+    for copy in ints + a_all + o_out + s_out:
         copy.wait_send()
-    for cond, copy in m_out + r_all:
+    for cond, copy in m_out + relays + r_all:
         if cond is None:
             copy.wait_send()
         else:
@@ -378,15 +427,15 @@
             pltpu.SMEM((own * slots * q2,), jnp.int32),
             pltpu.SMEM((own * slots * q2,), jnp.int32),
             pltpu.SMEM((own * q2,), jnp.int32),
-            dma((2 * chips,)), dma((blks,)),
-            dma((2 * chips,)), dma((2 * chips + 1,)),
+            dma((4 * chips,)), dma((2 * blks,)),
+            dma((4 * chips,)), dma((4 * chips + 2,)),
             dma((26,)), dma((4 * chips + 2,)),
             dma((blks,)), dma((blks,)), dma((3,)), dma((3,)), dma((3,)), dma((3,)),
             dma((blks,)), dma((blks,)), dma((blks,)), dma((blks,)),
-            dma((1,)), dma((2,)), dma((7,)),
+            dma((6,)), dma((2,)), dma((7,)),
         ],
         compiler_params=pltpu.CompilerParams(
-            collective_id=0, has_side_effects=True, vmem_limit_bytes=67043328
+            collective_id=0, has_side_effects=True, vmem_limit_bytes=66 * 10**6
         ),
     )(
         scol, cand.swapaxes(1, 2), rpat.swapaxes(1, 2), acol.T, mcol.swapaxes(1, 2), aval,

time: 79.1 us -> 74.5 us (0.942)
  Pallas kernels: 75.2 us -> 70.6 us
    pallas_call x1, Pallas kernels: 75.2 us -> 70.6 us  [on_device(): pl.pallas_call(functools.partial(kernel, dims), out_shape=(jax.ShapeDtype...]
where the time goes in v2:
time: 74.5 us; the launch traced here: 74.3 us
  Pallas kernels  70.6 us (95%)
  local copies, waits for them, and re-layouts  3.13 us (4%)
    pallas_call x1, Pallas kernels, on_device(): pl.pallas_call(functools.partial(kernel, dims), out_shape=(jax.ShapeDtype...  70.6 us
    unnamed x1, local copies, waits for them, and re-layouts  1.67 us

profile of v2, /device:TPU:1, one launch (start us, length us, event | category | flops | bytes accessed | tf_op | source)
XLA Modules:
  0.0 74.3 jit_solution(3468411169439477413)
XLA Ops:
  0.6 70.6 %shard_map.86 = (bf16[2,32,16,128]{3,2,1,0:T(8,128)(2,1)}, f32[2,4,8,128]{3,2,1,0:T(8,128)}) custom-call(s32[2,256]{1,0:T(2,128)} %scol_h.1, s32[2,2,16]{2,1,0:T(2,128)} %bitcast.13, s32[2,2,16]{2,1,0:T(2,128)} %bitcast.14, s32[4,16]{1,0:T(4,128)} %bitcast.15, s32[2,4,16]{2,1,0:T(4,128)} %bitcast.12, bf16[16,4,128,128]{3,2,1,0:T(8,128)(2,1)} %aval_h.1, ...), custom_call_target="tpu_custom_call" | custom-call | tf_op jit(solution)/shard_map/pallas_call | solution.py:405
  71.2 1.5 %constant_dynamic-slice_fusion = f32[2,4,8,16]{3,2,1,0:T(8,128)} fusion(f32[2,4,8,128]{3,2,1,0:T(8,128)} %get-tuple-element.5, s32[]{:T(128)S(6)} %select_n.3), kind=kLoop, calls=%fused_computation | loop fusion | bytes 8196 | tf_op jit(solution)/shard_map/dynamic_slice | solution.py:446
  72.7 1.7 %copy.10 = bf16[2,16,2,128,16]{3,4,2,1,0:T(8,128)(2,1)} copy(bf16[2,16,2,128,16]{3,4,2,1,0:T(8,128)(2,1)} %bitcast.10) | data formatting | bytes 524288

commit v3 on v2

--- a/solution.py
+++ b/solution.py
@@ -67,6 +67,26 @@
     r_win[zero_r] = jnp.zeros((n, n), r_win.dtype)
     pl.semaphore_wait(barrier, blks - 1 + 2)
 
+    hr = own // 2
+    hops = (1, chips - 1) + tuple(range(2, chips - 1))
+    a_all = []
+    a_rows = ((0, own - 1), (own - 1, 1))
+
+    def a_part(src, g):
+        return a_win.at[src, pl.ds(*a_rows[g])]
+
+    def a_copy(source, src, g, where):
+        copy = remote(
+            source, a_part(src, g), a_send.at[len(a_all)], a_recv.at[blks * g + src], where
+        )
+        copy.start()
+        a_all.append(copy)
+
+    def a_wait(src, g):
+        remote(
+            a_part(src, g), a_part(src, g), a_send.at[0], a_recv.at[blks * g + src], (r, b)
+        ).wait_recv()
+
     ints = []
     for d in range(1, blks):
         to = lax.rem(b + d, blks)
@@ -77,9 +97,15 @@
     for copy in ints:
         copy.start()
 
+
+    def a_start(g):
+        for d in hops:
+            a_copy(aval_h.at[pl.ds(own * across(d) + a_rows[g][0], a_rows[g][1])], b, g, (r, chip(d)))
+
+    a_start(0)
     last = chips - 1
     m_out = []
-    mh, hr = mq // 2, own // 2
+    mh = mq // 2
     for k in range(chips):
         for e in range(2):
             for cond, skip, j, h, slot, ring in (
@@ -99,31 +125,8 @@
                 )))
     for cond, copy in m_out:
         pl.when(cond)(copy.start)
-    hops = (1, chips - 1) + tuple(range(2, chips - 1))
-    a_all = []
-
-    def a_part(src, g):
-        return a_win.at[src, pl.ds(hr * g, hr)]
-
-    def a_copy(source, src, g, where):
-        copy = remote(
-            source, a_part(src, g), a_send.at[len(a_all)], a_recv.at[blks * g + src], where
-        )
-        copy.start()
-        a_all.append(copy)
-
-    def a_wait(src, g):
-        remote(
-            a_part(src, g), a_part(src, g), a_send.at[0], a_recv.at[blks * g + src], (r, b)
-        ).wait_recv()
-
-    for g in range(2):
-        for d in hops:
-            a_copy(aval_h.at[pl.ds(own * across(d) + hr * g, hr)], b, g, (r, chip(d)))
     home_a.wait()
-    for g in range(2):
-        a_copy(a_part(b, g), b, g, mate)
-
+    a_copy(a_part(b, 0), b, 0, mate)
     for copy in (home_ac, home_mc, home_rp, home_sc, home_ca):
         copy.wait()
     for d in range(1, blks):
@@ -211,6 +214,8 @@
             copy.start()
 
         pl.when(cond)(pass_on)
+    a_start(1)
+    a_copy(a_part(b, 1), b, 1, mate)
 
     def a_swap(g):
         for d in hops:
@@ -273,7 +278,8 @@
             r_turn[q2 * i + p] = block.T.astype(r_turn.dtype)
         return carry
 
-    rh = rq // 2
+    pieces = own
+    rh = rq // pieces
     r_all = []
 
     def piece(slot, h):
@@ -284,7 +290,7 @@
             to_slot = jnp.clip(to_slot, 0, 2 * chips)
         copy = remote(
             piece(slot, h), piece(to_slot, h), r_send.at[len(r_all)],
-            r_recv.at[2 * to_slot + h], where,
+            r_recv.at[pieces * to_slot + h], where,
         )
         r_all.append((cond, copy))
         if cond is None:
@@ -295,7 +301,7 @@
     def take(slot, h, cond=None):
         def wait():
             remote(
-                piece(slot, h), piece(slot, h), r_send.at[0], r_recv.at[2 * slot + h], (r, b)
+                piece(slot, h), piece(slot, h), r_send.at[0], r_recv.at[pieces * slot + h], (r, b)
             ).wait_recv()
 
         if cond is None:
@@ -303,35 +309,35 @@
         else:
             pl.when(cond)(wait)
 
-    for h in range(2):
-        if h == 1:
+    for h in range(pieces):
+        if h == a_rows[1][0]:
             a_swap(1)
-        lax.fori_loop(own // 2 * h, own // 2 * (h + 1), resid_row, 0)
+        resid_row(h, 0)
         give(chips, h, chips + x - right, by_right)
         give(chips, h, chips + x - left, by_left)
         give(chips, h, 0, above)
         give(chips, h, 2 * chips, below)
 
     at_left, at_right = chips + left - x, chips + right - x
-    for h in range(2):
+    for h in range(pieces):
         take(at_left, h)
-        if h == 0:
+        if h < hr:
             give(at_left, h, chips + left - right, by_right)
         give(at_left, h, 2 * chips - 1, below, x >= 1)
         take(at_right, h)
-        if h == 1:
+        if h >= hr:
             give(at_right, h, chips + right - left, by_left)
         give(at_right, h, 1, above, x <= last - 1)
         take(0, h)
         give(0, h, last, by_right, x == last)
         take(2 * chips, h)
         give(2 * chips, h, chips + 1, by_left, x == 0)
-    for h in range(2):
+    for h in range(pieces):
         take(1, h, x <= last - 1)
         give(1, h, 2, by_left, inner)
         take(2 * chips - 1, h, x >= 1)
         give(2 * chips - 1, h, 2 * chips - 2, by_right, inner)
-    for h in range(2):
+    for h in range(pieces):
         take(jnp.where(x < 2, chips + 2, chips - 2), h)
         take(2, h, x < 2)
         take(3, h, x == 0)
@@ -364,13 +370,21 @@
     home_s = pltpu.make_async_copy(sc_own, o_sc.at[t, x], loc.at[1])
     home_s.start()
     s_out = []
-    for d in range(1, blks):
+    for d in (4, 3, 5, 2, 6, 7, 1):
         to = lax.rem(b + d, blks)
         s_out.append(remote(
             sc_own, o_sc.at[t, x], s_send.at[d], s_recv.at[b], (r, to)
         ))
         s_out[-1].start()
 
+    for copy in ints + a_all + o_out + s_out:
+        copy.wait_send()
+    for cond, copy in m_out + relays + r_all:
+        if cond is None:
+            copy.wait_send()
+        else:
+            pl.when(cond)(copy.wait_send)
+    home_o.wait()
     for d in range(1, blks):
         src = lax.rem(b + d, blks)
         sx, st = src // CORES, src % CORES
@@ -379,15 +393,7 @@
             o_send.at[d], o_recv.at[src], (r, b),
         ).wait_recv()
         remote(sc_own, o_sc.at[st, sx], s_send.at[d], s_recv.at[src], (r, b)).wait_recv()
-    home_o.wait()
     home_s.wait()
-    for copy in ints + a_all + o_out + s_out:
-        copy.wait_send()
-    for cond, copy in m_out + relays + r_all:
-        if cond is None:
-            copy.wait_send()
-        else:
-            pl.when(cond)(copy.wait_send)
 
 
 def on_device(rings, blks, acol, aval, mcol, mval, rpat, scol, cand):
@@ -429,7 +435,7 @@
             pltpu.SMEM((own * q2,), jnp.int32),
             dma((4 * chips,)), dma((2 * blks,)),
             dma((4 * chips,)), dma((4 * chips + 2,)),
-            dma((26,)), dma((4 * chips + 2,)),
+            dma((11 * own,)), dma(((2 * chips + 1) * own,)),
             dma((blks,)), dma((blks,)), dma((3,)), dma((3,)), dma((3,)), dma((3,)),
             dma((blks,)), dma((blks,)), dma((blks,)), dma((blks,)),
             dma((6,)), dma((2,)), dma((7,)),
@@ -441,10 +447,24 @@
         scol, cand.swapaxes(1, 2), rpat.swapaxes(1, 2), acol.T, mcol.swapaxes(1, 2), aval,
         mval.reshape(slabs, rows * qm, n, n),
     )
-    start = lax.axis_index("blk") * width
+    def finish(res_ref, sc_ref, o_ref, s_ref):
+        b = lax.axis_index("blk")
+        o_ref[...] = res_ref[...]
+        for k in range(blks):
+
+            @pl.when(b == k)
+            def _():
+                s_ref[...] = sc_ref[:, width * k:width * (k + 1)]
+
+    res, sc = pl.pallas_call(
+        finish,
+        out_shape=(
+            jax.ShapeDtypeStruct((slabs * rows * q2 * width, n), jnp.bfloat16),
+            jax.ShapeDtypeStruct((slabs * rows * q2, width), jnp.float32),
+        ),
+    )(res.reshape(-1, n), sc.reshape(-1, n))
     resid = res.reshape(slabs, rows, q2, width, n).swapaxes(3, 4)
-    scores = lax.dynamic_slice_in_dim(sc, start, width, 3).reshape(slabs, rows, q2, width)
-    return resid, scores
+    return resid, sc.reshape(slabs, rows, q2, width)
 
 
 def solution(mesh):

time: 74.5 us -> 70.2 us (0.942)
  local copies, waits for them, and re-layouts: 3.13 us -> 0 us
  Pallas kernels: 70.6 us -> 69.5 us
    pallas_call x1, Pallas kernels: 70.6 us -> 67.7 us  [on_device(): pl.pallas_call(functools.partial(kernel, dims), out_shape=(jax.ShapeDtype...]
    pallas_call x0 -> x1, Pallas kernels: none -> 1.75 us  [on_device(): pl.pallas_call(finish, out_shape=(jax.ShapeDtypeStruct((slabs * rows * q2...]
    unnamed x1 -> x0, local copies, waits for them, and re-layouts: 1.67 us -> none
    dynamic_slice x1 -> x0, local copies, waits for them, and re-layouts: 1.46 us -> none  [on_device(): lax.dynamic_slice_in_dim(sc, start, width, 3)]
where the time goes in v3:
time: 70.2 us; the launch traced here: 70.1 us
  Pallas kernels  69.5 us (99%)
    pallas_call x1, Pallas kernels, on_device(): pl.pallas_call(functools.partial(kernel, dims), out_shape=(jax.ShapeDtype...  67.7 us
    pallas_call x1, Pallas kernels, on_device(): pl.pallas_call(finish, out_shape=(jax.ShapeDtypeStruct((slabs * rows * q2...  1.75 us

profile of v3, /device:TPU:1, one launch (start us, length us, event | category | flops | bytes accessed | tf_op | source)
XLA Modules:
  0.0 70.1 jit_solution(7201884059767779194)
XLA Ops:
  0.6 67.7 %shard_map.86 = (bf16[2,32,16,128]{3,2,1,0:T(8,128)(2,1)}, f32[2,4,8,128]{3,2,1,0:T(8,128)}) custom-call(s32[2,256]{1,0:T(2,128)} %scol_h.1, s32[2,2,16]{2,1,0:T(2,128)} %bitcast.15, s32[2,2,16]{2,1,0:T(2,128)} %bitcast.16, s32[4,16]{1,0:T(4,128)} %bitcast.17, s32[2,4,16]{2,1,0:T(4,128)} %bitcast.14, bf16[16,4,128,128]{3,2,1,0:T(8,128)(2,1)} %aval_h.1, ...), custom_call_target="tpu_custom_call" | custom-call | tf_op jit(solution)/shard_map/pallas_call | solution.py:411
  68.4 1.8 %shard_map.87 = (bf16[1024,128]{1,0:T(8,128)(2,1)}, f32[64,16]{1,0:T(8,128)}) custom-call(bf16[1024,128]{1,0:T(8,128)(2,1)} %bitcast.12, f32[64,128]{1,0:T(8,128)} %bitcast.13), custom_call_target="tpu_custom_call" | custom-call | tf_op jit(solution)/shard_map/pallas_call | solution.py:459

commit v4 on v3

--- a/solution.py
+++ b/solution.py
@@ -61,11 +61,16 @@
         pl.semaphore_signal(
             barrier, inc=1, device_id=(r, lax.rem(b + d, blks)), device_id_type=MESH
         )
+    left, right = lax.rem(x + chips - 1, chips), lax.rem(x + 1, chips)
+    for ring, side in ((up, left), (down, right)):
+        pl.semaphore_signal(
+            barrier, inc=1, device_id=(ring, CORES * side + t), device_id_type=MESH
+        )
     for copy in (home_ac, home_mc, home_rp, home_sc, home_ca, home_a, home_m):
         copy.start()
     m_win[zero_m] = jnp.zeros((n, n), m_win.dtype)
     r_win[zero_r] = jnp.zeros((n, n), r_win.dtype)
-    pl.semaphore_wait(barrier, blks - 1 + 2)
+    pl.semaphore_wait(barrier, blks - 1 + 4)
 
     hr = own // 2
     hops = (1, chips - 1) + tuple(range(2, chips - 1))
@@ -178,7 +183,6 @@
 
     lax.fori_loop(0, own, table_row, 0)
 
-    left, right = lax.rem(x + last, chips), lax.rem(x + 1, chips)
     by_left, by_right = (r, CORES * left + t), (r, CORES * right + t)
     above, below = (up, b), (down, b)
     inner = (x >= 1) & (x <= last - 1)
@@ -275,10 +279,9 @@
         for p in range(q2):
             block = summed[:, n * p:n * (p + 1)] - diag[q2 * i + p].astype(jnp.float32) * eye
             r_win[rq * chips + q2 * i + p] = block.astype(r_win.dtype)
-            r_turn[q2 * i + p] = block.T.astype(r_turn.dtype)
         return carry
 
-    pieces = own
+    pieces, direct = own, own - 1
     rh = rq // pieces
     r_all = []
 
@@ -318,25 +321,40 @@
         give(chips, h, 0, above)
         give(chips, h, 2 * chips, below)
 
+    for k in range(rq):
+        block = r_win[rq * chips + k].astype(jnp.float32)
+        r_turn[k] = block.T.astype(r_turn.dtype)
+
     at_left, at_right = chips + left - x, chips + right - x
     for h in range(pieces):
         take(at_left, h)
         if h < hr:
             give(at_left, h, chips + left - right, by_right)
         give(at_left, h, 2 * chips - 1, below, x >= 1)
+        if h >= direct:
+            give(at_left, h, 2 * chips - 2, (down, CORES * right + t), inner)
         take(at_right, h)
         if h >= hr:
             give(at_right, h, chips + right - left, by_left)
         give(at_right, h, 1, above, x <= last - 1)
+        if h >= direct:
+            give(at_right, h, 2, (up, CORES * left + t), inner)
+        if h >= direct:
+            give(at_left, h, last, above, x == 0)
+            give(at_right, h, chips + 1, below, x == last)
         take(0, h)
-        give(0, h, last, by_right, x == last)
+        if h < direct:
+            give(0, h, last, by_right, x == last)
         take(2 * chips, h)
-        give(2 * chips, h, chips + 1, by_left, x == 0)
+        if h < direct:
+            give(2 * chips, h, chips + 1, by_left, x == 0)
     for h in range(pieces):
         take(1, h, x <= last - 1)
-        give(1, h, 2, by_left, inner)
+        if h < direct:
+            give(1, h, 2, by_left, inner)
         take(2 * chips - 1, h, x >= 1)
-        give(2 * chips - 1, h, 2 * chips - 2, by_right, inner)
+        if h < direct:
+            give(2 * chips - 1, h, 2 * chips - 2, by_right, inner)
     for h in range(pieces):
         take(jnp.where(x < 2, chips + 2, chips - 2), h)
         take(2, h, x < 2)

time: 70.2 us -> 69.1 us (0.984)
  Pallas kernels: 69.5 us -> 68.4 us
    pallas_call x1, Pallas kernels: 67.7 us -> 66.6 us  [on_device(): pl.pallas_call(functools.partial(kernel, dims), out_shape=(jax.ShapeDtype...]
where the time goes in v4:
time: 69.1 us; the launch traced here: 69 us
  Pallas kernels  68.4 us (99%)
    pallas_call x1, Pallas kernels, on_device(): pl.pallas_call(functools.partial(kernel, dims), out_shape=(jax.ShapeDtype...  66.6 us
    pallas_call x1, Pallas kernels, on_device(): pl.pallas_call(finish, out_shape=(jax.ShapeDtypeStruct((slabs * rows * q2...  1.75 us

profile of v4, /device:TPU:1, one launch (start us, length us, event | category | flops | bytes accessed | tf_op | source)
XLA Modules:
  0.0 69.0 jit_solution(6600834518029124413)
XLA Ops:
  0.6 66.6 %shard_map.86 = (bf16[2,32,16,128]{3,2,1,0:T(8,128)(2,1)}, f32[2,4,8,128]{3,2,1,0:T(8,128)}) custom-call(s32[2,256]{1,0:T(2,128)} %scol_h.1, s32[2,2,16]{2,1,0:T(2,128)} %bitcast.15, s32[2,2,16]{2,1,0:T(2,128)} %bitcast.16, s32[4,16]{1,0:T(4,128)} %bitcast.17, s32[2,4,16]{2,1,0:T(4,128)} %bitcast.14, bf16[16,4,128,128]{3,2,1,0:T(8,128)(2,1)} %aval_h.1, ...), custom_call_target="tpu_custom_call" | custom-call | tf_op jit(solution)/shard_map/pallas_call | solution.py:429
  67.3 1.8 %shard_map.87 = (bf16[1024,128]{1,0:T(8,128)(2,1)}, f32[64,16]{1,0:T(8,128)}) custom-call(bf16[1024,128]{1,0:T(8,128)(2,1)} %bitcast.12, f32[64,128]{1,0:T(8,128)} %bitcast.13), custom_call_target="tpu_custom_call" | custom-call | tf_op jit(solution)/shard_map/pallas_call | solution.py:477

commit v5 on v4

--- a/solution.py
+++ b/solution.py
@@ -342,11 +342,10 @@
         if h >= direct:
             give(at_left, h, last, above, x == 0)
             give(at_right, h, chips + 1, below, x == last)
-        take(0, h)
         if h < direct:
+            take(0, h, x == last)
             give(0, h, last, by_right, x == last)
-        take(2 * chips, h)
-        if h < direct:
+            take(2 * chips, h, x == 0)
             give(2 * chips, h, chips + 1, by_left, x == 0)
     for h in range(pieces):
         take(1, h, x <= last - 1)
@@ -356,6 +355,8 @@
         if h < direct:
             give(2 * chips - 1, h, 2 * chips - 2, by_right, inner)
     for h in range(pieces):
+        take(0, h, None if h == direct else x != last)
+        take(2 * chips, h, None if h == direct else x != 0)
         take(jnp.where(x < 2, chips + 2, chips - 2), h)
         take(2, h, x < 2)
         take(3, h, x == 0)

time: 69.1 us -> 69 us (level)
  no operation moved by 1% of the time
where the time goes in v5:
time: 69 us; the launch traced here: 68.9 us
  Pallas kernels  68.2 us (99%)
    pallas_call x1, Pallas kernels, on_device(): pl.pallas_call(functools.partial(kernel, dims), out_shape=(jax.ShapeDtype...  66.5 us
    pallas_call x1, Pallas kernels, on_device(): pl.pallas_call(finish, out_shape=(jax.ShapeDtypeStruct((slabs * rows * q2...  1.75 us

profile of v5, /device:TPU:1, one launch (start us, length us, event | category | flops | bytes accessed | tf_op | source)
XLA Modules:
  0.0 68.9 jit_solution(7159039466844513811)
XLA Ops:
  0.6 66.5 %shard_map.86 = (bf16[2,32,16,128]{3,2,1,0:T(8,128)(2,1)}, f32[2,4,8,128]{3,2,1,0:T(8,128)}) custom-call(s32[2,256]{1,0:T(2,128)} %scol_h.1, s32[2,2,16]{2,1,0:T(2,128)} %bitcast.15, s32[2,2,16]{2,1,0:T(2,128)} %bitcast.16, s32[4,16]{1,0:T(4,128)} %bitcast.17, s32[2,4,16]{2,1,0:T(4,128)} %bitcast.14, bf16[16,4,128,128]{3,2,1,0:T(8,128)(2,1)} %aval_h.1, ...), custom_call_target="tpu_custom_call" | custom-call | tf_op jit(solution)/shard_map/pallas_call | solution.py:430
  67.1 1.8 %shard_map.87 = (bf16[1024,128]{1,0:T(8,128)(2,1)}, f32[64,16]{1,0:T(8,128)}) custom-call(bf16[1024,128]{1,0:T(8,128)(2,1)} %bitcast.12, f32[64,128]{1,0:T(8,128)} %bitcast.13), custom_call_target="tpu_custom_call" | custom-call | tf_op jit(solution)/shard_map/pallas_call | solution.py:478

commit v6 on v5

--- a/solution.py
+++ b/solution.py
@@ -107,7 +107,6 @@
         for d in hops:
             a_copy(aval_h.at[pl.ds(own * across(d) + a_rows[g][0], a_rows[g][1])], b, g, (r, chip(d)))
 
-    a_start(0)
     last = chips - 1
     m_out = []
     mh = mq // 2
@@ -130,6 +129,7 @@
                 )))
     for cond, copy in m_out:
         pl.when(cond)(copy.start)
+    a_start(0)
     home_a.wait()
     a_copy(a_part(b, 0), b, 0, mate)
     for copy in (home_ac, home_mc, home_rp, home_sc, home_ca):

time: 69 us -> 69 us (level)
  no operation moved by 1% of the time
where the time goes in v6:
time: 69 us; the launch traced here: 68.9 us
  Pallas kernels  68.2 us (99%)
    pallas_call x1, Pallas kernels, on_device(): pl.pallas_call(functools.partial(kernel, dims), out_shape=(jax.ShapeDtype...  66.5 us
    pallas_call x1, Pallas kernels, on_device(): pl.pallas_call(finish, out_shape=(jax.ShapeDtypeStruct((slabs * rows * q2...  1.75 us

profile of v6, /device:TPU:1, one launch (start us, length us, event | category | flops | bytes accessed | tf_op | source)
XLA Modules:
  0.0 68.9 jit_solution(8545098299196647267)
XLA Ops:
  0.6 66.5 %shard_map.86 = (bf16[2,32,16,128]{3,2,1,0:T(8,128)(2,1)}, f32[2,4,8,128]{3,2,1,0:T(8,128)}) custom-call(s32[2,256]{1,0:T(2,128)} %scol_h.1, s32[2,2,16]{2,1,0:T(2,128)} %bitcast.15, s32[2,2,16]{2,1,0:T(2,128)} %bitcast.16, s32[4,16]{1,0:T(4,128)} %bitcast.17, s32[2,4,16]{2,1,0:T(4,128)} %bitcast.14, bf16[16,4,128,128]{3,2,1,0:T(8,128)(2,1)} %aval_h.1, ...), custom_call_target="tpu_custom_call" | custom-call | tf_op jit(solution)/shard_map/pallas_call | solution.py:430
  67.1 1.8 %shard_map.87 = (bf16[1024,128]{1,0:T(8,128)(2,1)}, f32[64,16]{1,0:T(8,128)}) custom-call(bf16[1024,128]{1,0:T(8,128)(2,1)} %bitcast.12, f32[64,128]{1,0:T(8,128)} %bitcast.13), custom_call_target="tpu_custom_call" | custom-call | tf_op jit(solution)/shard_map/pallas_call | solution.py:478
